TPU v7x, 512 devices: a whole 4x4x16 slice. The times are simulated.
512 devices in a mesh: fsdp: 16 (over x, y), dp: 32 (over z, core).
Axes of the slice: x: 4, y: 4, z: 16, core: 2. Of those that a mesh axis runs over, the one named last changes fastest.
Arguments:
- tokens: bfloat16 [65536, 4096], P(('fsdp', 'dp')), may hold values from -6 to 6
- master_old: float32 [512, 128, 128], P(('fsdp', 'dp')), may hold values from -0.25 to 0.25
- moment_old: float32 [512, 128, 128], P(('fsdp', 'dp')), may hold values from -6 to 6
- second_old: float32 [512, 128, 128], P(('fsdp', 'dp')), may hold values from 0.01 to 1
- old_cell: int32 [112, 4], P('fsdp'), may hold values from 0 to 31, as said below
- new_cell: int32 [112, 4], P('fsdp'), may hold values from 0 to 31, as said below
- regrown: int32 [112, 4], P('fsdp'), may hold values 0 or 1
- new_rows: int32 [112, 4], replicated, may hold values from 0 to 31, as said below
Outputs:
- hidden: bfloat16 [65536, 14336], P(('fsdp', 'dp'))
- master_new: float32 [512, 128, 128], P(('fsdp', 'dp'))
- moment_new: float32 [512, 128, 128], P(('fsdp', 'dp'))
- second_new: float32 [512, 128, 128], P(('fsdp', 'dp'))
Inputs may be any that keep to these rules, and one draw needn't show every extreme that they name: `old_cell`: within one fsdp index, taking its slots column by column and then by k, the old cells strictly increase; a cell's index // 1 is its holder along dp and index % 1 its place in that holder's buffer. `new_cell`: strictly increasing in the same order; every slot's new cell differs from its old cell by at most 4, and by exactly 4 for some slot of every fsdp index. `new_rows`: the 4 block rows of one block column are distinct.
All inputs are finite; a program needn't handle non-finite values. No bound on the sum of `regrown` on one device may be relied on, other than what follows from the above.
Results may differ from a plain program's by a relative error of at most 0.007.
Values may be sent and summed in bfloat16 or wider, within the bound.
No kernel may reach another device: no remote copies, remote signals or barrier semaphores. Data moves between devices by JAX's collectives and lax.ppermute only.
A program may use at most 128 MiB of HBM per device.

v0:
```python
import jax
import jax.numpy as jnp
from jax import lax
from jax.sharding import PartitionSpec as P


def passed_along(block, axis, distance):
    devices = range(lax.axis_size(axis))
    route = [(i - distance, i) for i in devices if i - distance in devices]
    return lax.ppermute(block, axis, route)


def on_device(tokens, master_old, moment_old, second_old, old_cell, new_cell, regrown, new_rows):
    block_size = master_old.shape[1]
    capacity = master_old.shape[0]
    column_count = old_cell.shape[0]
    nonzero_count = old_cell.shape[1]
    slot_count = column_count * nonzero_count
    axis_width = lax.axis_size("dp")
    cell_count = axis_width * capacity
    farthest = min((cell_count - slot_count + capacity - 1) // capacity, axis_width - 1)
    holder = lax.axis_index("dp")
    old_flat = old_cell.reshape(-1)
    new_flat = new_cell.reshape(-1)
    keep_flag = regrown.reshape(-1) == 0
    my_cells = holder * capacity + jnp.arange(capacity, dtype=jnp.int32)
    matches = new_flat[None, :] == my_cells[:, None]
    present = jnp.any(matches & keep_flag[None, :], axis=1)
    source = jnp.sum(jnp.where(matches, old_flat[None, :], 0), axis=1)
    offset = holder - source // capacity
    slot_place = source % capacity
    candidate = jnp.where(offset > 0, 2 * offset - 1, jnp.where(offset < 0, -2 * offset, 0))
    pick_index = candidate * capacity + slot_place
    own_states = (master_old, moment_old, second_old)
    shift_list = []
    for distance in range(1, farthest + 1):
        shift_list.append(distance)
        shift_list.append(-distance)
    received_list = [own_states]
    for by_value in shift_list:
        received_list.append(
            (
                passed_along(own_states[0].astype(jnp.bfloat16), "dp", by_value).astype(
                    jnp.float32
                ),
                passed_along(own_states[1].astype(jnp.bfloat16), "dp", by_value).astype(
                    jnp.float32
                ),
                passed_along(own_states[2].astype(jnp.bfloat16), "dp", by_value).astype(
                    jnp.float32
                ),
            )
        )

    def settle(member):
        pool = jnp.concatenate([entry[member] for entry in received_list], axis=0)
        chosen = jnp.take(pool, pick_index, axis=0, mode="clip")
        return jnp.where(present[:, None, None], chosen, jnp.float32(0.0))

    master_new = settle(0)
    moment_new = settle(1)
    second_new = settle(2)
    cell_blocks = master_new.astype(jnp.bfloat16)
    group_cells = lax.all_gather(cell_blocks, "dp", axis=0, tiled=True)
    panel = jnp.take(group_cells, new_flat, axis=0).reshape(
        column_count, nonzero_count, block_size, block_size
    )
    token_count = tokens.shape[0]
    token_blocks = tokens.reshape(token_count, tokens.shape[1] // block_size, block_size)
    panel_piece = lax.all_gather(panel, "fsdp", axis=0, tiled=True)
    count = panel_piece.shape[0]
    picked = jnp.take(token_blocks, new_rows.reshape(-1), axis=1)
    picked = picked.reshape(token_count, count, nonzero_count, block_size)
    product = jnp.einsum("tcka,ckab->tcb", picked, panel_piece, preferred_element_type=jnp.float32)
    hidden = product.reshape(token_count, count * block_size).astype(jnp.bfloat16)
    return (hidden, master_new, moment_new, second_new)


def solution(mesh):
    return jax.shard_map(
        on_device,
        mesh=mesh,
        in_specs=(
            P(("fsdp", "dp"), None),
            P(("fsdp", "dp"), None, None),
            P(("fsdp", "dp"), None, None),
            P(("fsdp", "dp"), None, None),
            P("fsdp", None),
            P("fsdp", None),
            P("fsdp", None),
            P(),
        ),
        out_specs=(
            P(("fsdp", "dp"), None),
            P(("fsdp", "dp"), None, None),
            P(("fsdp", "dp"), None, None),
            P(("fsdp", "dp"), None, None),
        ),
        check_vma=False,
    )
```

profile of v0, /device:TPU:1, one launch (start us, length us, event | category | flops | bytes accessed | tf_op | source)
XLA Modules:
  0.0 264.1 jit_solution(16962180668199227297)
XLA Ops:
  7.2 0.9 fusion.11
  8.1 4.9 %collective-permute-start = (bf16[1,128,128]{2,1,0:T(8,128)(2,1)S(1)}, bf16[1,128,128]{2,1,0:T(8,128)(2,1)S(1)}, u32[]{:S(2)}, u32[]{:S(2)}) collective-permute-start(bf16[1,128,128]{2,1,0:T(8,128)(2,1)S(1)} %get-tuple-element.61), channel_id=1, source_target_pairs={{0,1},{1,2},{2,3},{3,4},{4,5},{5,6},{6,7},{7,8},{8,9},{9,10},{10,1... | collective-permute-start | bytes 98312 | tf_op jit(solution)/shard_map/ppermute | solution.py:10
  13.1 5.1 %collective-permute-start.1 = (bf16[1,128,128]{2,1,0:T(8,128)(2,1)S(1)}, bf16[1,128,128]{2,1,0:T(8,128)(2,1)S(1)}, u32[]{:S(2)}, u32[]{:S(2)}) collective-permute-start(bf16[1,128,128]{2,1,0:T(8,128)(2,1)S(1)} %get-tuple-element.61), channel_id=1, source_target_pairs={{1,0},{2,1},{3,2},{4,3},{5,4},{6,5},{7,6},{8,7},{9,8},{10,9},{11,1... | collective-permute-start | bytes 98312 | tf_op jit(solution)/shard_map/ppermute | solution.py:10
  18.2 1.3 collective-permute-start.2
  19.5 1.3 collective-permute-start.3
  20.8 5.0 %collective-permute-start.4 = (bf16[1,128,128]{2,1,0:T(8,128)(2,1)S(1)}, bf16[1,128,128]{2,1,0:T(8,128)(2,1)S(1)}, u32[]{:S(2)}, u32[]{:S(2)}) collective-permute-start(bf16[1,128,128]{2,1,0:T(8,128)(2,1)S(1)} %get-tuple-element.61), channel_id=1, source_target_pairs={{0,3},{1,4},{2,5},{3,6},{4,7},{5,8},{6,9},{7,10},{8,11},{9,12},{10... | collective-permute-start | bytes 98312 | tf_op jit(solution)/shard_map/ppermute | solution.py:10
  25.9 1.4 and_reduce_fusion
  27.3 1.3 select_reduce_fusion
  29.3 1.3 collective-permute-start.5
  30.6 9.2 %collective-permute-start.6 = (bf16[1,128,128]{2,1,0:T(8,128)(2,1)S(1)}, bf16[1,128,128]{2,1,0:T(8,128)(2,1)S(1)}, u32[]{:S(2)}, u32[]{:S(2)}) collective-permute-start(bf16[1,128,128]{2,1,0:T(8,128)(2,1)S(1)} %get-tuple-element.61), channel_id=1, source_target_pairs={{0,4},{1,5},{2,6},{3,7},{4,8},{5,9},{6,10},{7,11},{8,12},{9,13},{1... | collective-permute-start | bytes 98312 | tf_op jit(solution)/shard_map/ppermute | solution.py:10
  39.8 1.3 collective-permute-start.7
  41.2 4.1 %collective-permute-done.7 = bf16[1,128,128]{2,1,0:T(8,128)(2,1)S(1)} collective-permute-done((bf16[1,128,128]{2,1,0:T(8,128)(2,1)S(1)}, bf16[1,128,128]{2,1,0:T(8,128)(2,1)S(1)}, u32[]{:S(2)}, u32[]{:S(2)}) %collective-permute-start.7) | collective-permute-done | bytes 32800 | tf_op jit(solution)/shard_map/ppermute | solution.py:10
  45.3 1.3 fusion.8
  46.7 0.8 copy.33
  47.5 0.1 copy.32
  47.7 73.8 %all-gather.3.cloned.1.call-done = bf16[32,128,128]{2,1,0:T(8,128)(2,1)} async-done(((bf16[1,128,128]{2,1,0:T(8,128)(2,1)}), bf16[32,128,128]{2,1,0:T(8,128)(2,1)}) %all-gather.3.cloned.1.call-update) | async-done | bytes 1048592 | tf_op jit(solution)/shard_map/all_gather | solution.py:64
  121.4 1.9 gather_fusion
  123.4 1.1 broadcast_select_fusion
  124.5 0.9 fusion.9
  125.4 3.2 %collective-permute-start.16 = (bf16[1,128,128]{2,1,0:T(8,128)(2,1)S(1)}, bf16[1,128,128]{2,1,0:T(8,128)(2,1)S(1)}, u32[]{:S(2)}, u32[]{:S(2)}) collective-permute-start(bf16[1,128,128]{2,1,0:T(8,128)(2,1)S(1)} %get-tuple-element.57), channel_id=1, source_target_pairs={{0,1},{1,2},{2,3},{3,4},{4,5},{5,6},{6,7},{7,8},{8,9},{9,10},{10,1... | collective-permute-start | bytes 98312 | tf_op jit(solution)/shard_map/ppermute | solution.py:10
  128.6 1.9 collective-permute-start.17
  130.5 2.3 collective-permute-start.18
  132.8 1.3 collective-permute-start.19
  134.1 6.0 %collective-permute-start.20 = (bf16[1,128,128]{2,1,0:T(8,128)(2,1)S(1)}, bf16[1,128,128]{2,1,0:T(8,128)(2,1)S(1)}, u32[]{:S(2)}, u32[]{:S(2)}) collective-permute-start(bf16[1,128,128]{2,1,0:T(8,128)(2,1)S(1)} %get-tuple-element.57), channel_id=1, source_target_pairs={{0,3},{1,4},{2,5},{3,6},{4,7},{5,8},{6,9},{7,10},{8,11},{9,12},{10... | collective-permute-start | bytes 98312 | tf_op jit(solution)/shard_map/ppermute | solution.py:10
  140.1 0.8 copy.36
  141.0 0.7 compare_and_fusion
  141.7 0.9 fusion.10
  142.7 1.6 copy.35
  144.3 0.7 copy.37
  145.0 0.1 copy.34
  145.1 13.3 %gather_fusion.1 = bf16[448,128,128]{2,1,0:T(8,128)(2,1)} fusion(bf16[128,32,128]{2,0,1:T(8,128)(2,1)S(1)} %copy.37, s32[1024]{0:T(1024)S(1)} %pad_clamp_fusion), kind=kCustom, calls=%fused_computation.1 | custom fusion | bytes 29361920 | tf_op jit(solution)/shard_map/jit(_take)/gather | solution.py:72
  158.4 1.3 collective-permute-start.21
  159.7 6.6 %collective-permute-start.22 = (bf16[1,128,128]{2,1,0:T(8,128)(2,1)S(1)}, bf16[1,128,128]{2,1,0:T(8,128)(2,1)S(1)}, u32[]{:S(2)}, u32[]{:S(2)}) collective-permute-start(bf16[1,128,128]{2,1,0:T(8,128)(2,1)S(1)} %get-tuple-element.57), channel_id=1, source_target_pairs={{0,4},{1,5},{2,6},{3,7},{4,8},{5,9},{6,10},{7,11},{8,12},{9,13},{1... | collective-permute-start | bytes 98312 | tf_op jit(solution)/shard_map/ppermute | solution.py:10
  166.3 1.3 collective-permute-start.23
  167.6 2.2 collective-permute-start.8
  169.8 2.2 collective-permute-start.9
  172.0 6.4 %collective-permute-start.10 = (bf16[1,128,128]{2,1,0:T(8,128)(2,1)S(1)}, bf16[1,128,128]{2,1,0:T(8,128)(2,1)S(1)}, u32[]{:S(2)}, u32[]{:S(2)}) collective-permute-start(bf16[1,128,128]{2,1,0:T(8,128)(2,1)S(1)} %get-tuple-element.59), channel_id=1, source_target_pairs={{0,2},{1,3},{2,4},{3,5},{4,6},{5,7},{6,8},{7,9},{8,10},{9,11},{10,... | collective-permute-start | bytes 98312 | tf_op jit(solution)/shard_map/ppermute | solution.py:10
  178.5 1.3 collective-permute-start.11
  179.8 6.0 %collective-permute-start.12 = (bf16[1,128,128]{2,1,0:T(8,128)(2,1)S(1)}, bf16[1,128,128]{2,1,0:T(8,128)(2,1)S(1)}, u32[]{:S(2)}, u32[]{:S(2)}) collective-permute-start(bf16[1,128,128]{2,1,0:T(8,128)(2,1)S(1)} %get-tuple-element.59), channel_id=1, source_target_pairs={{0,3},{1,4},{2,5},{3,6},{4,7},{5,8},{6,9},{7,10},{8,11},{9,12},{10... | collective-permute-start | bytes 98312 | tf_op jit(solution)/shard_map/ppermute | solution.py:10
  185.9 1.3 collective-permute-start.13
  187.2 8.8 %collective-permute-start.14 = (bf16[1,128,128]{2,1,0:T(8,128)(2,1)S(1)}, bf16[1,128,128]{2,1,0:T(8,128)(2,1)S(1)}, u32[]{:S(2)}, u32[]{:S(2)}) collective-permute-start(bf16[1,128,128]{2,1,0:T(8,128)(2,1)S(1)} %get-tuple-element.59), channel_id=1, source_target_pairs={{0,4},{1,5},{2,6},{3,7},{4,8},{5,9},{6,10},{7,11},{8,12},{9,13},{1... | collective-permute-start | bytes 98312 | tf_op jit(solution)/shard_map/ppermute | solution.py:10
  196.0 1.3 collective-permute-start.15
  197.5 1.3 dynamic-slice_select_fusion
  198.7 3.3 %collective-permute-done.15 = bf16[1,128,128]{2,1,0:T(8,128)(2,1)S(1)} collective-permute-done((bf16[1,128,128]{2,1,0:T(8,128)(2,1)S(1)}, bf16[1,128,128]{2,1,0:T(8,128)(2,1)S(1)}, u32[]{:S(2)}, u32[]{:S(2)}) %collective-permute-start.15) | collective-permute-done | bytes 32800 | tf_op jit(solution)/shard_map/ppermute | solution.py:10
  202.0 1.3 dynamic-slice_select_fusion.1
  203.3 34.5 %all-gather.5.cloned.1.call-done = bf16[112,4,128,128]{3,2,1,0:T(8,128)(2,1)} async-done(((bf16[7,4,128,128]{3,2,1,0:T(8,128)(2,1)}), bf16[112,4,128,128]{3,2,1,0:T(8,128)(2,1)}) %all-gather.5.cloned.1.call-update) | async-done | bytes 14680080 | tf_op jit(solution)/shard_map/all_gather | solution.py:70
  237.7 13.5 %bitcast_convert_fusion = bf16[112,128,128]{2,1,0:T(8,128)(2,1)} fusion(bf16[112,4,128,128]{3,2,1,0:T(8,128)(2,1)} %all-gather.5.cloned.1.call-done, bf16[128,112,4,128]{3,0,2,1:T(8,128)(2,1)} %bitcast.15, pred[112,4]{1,0:T(8,128)(4,1)S(1)} %copy.34), kind=kOutput, calls=%fused_computation.5 | convolution fusion | flops 1888223232 | bytes 33030592 | tf_op jit(solution)/shard_map/tcka,ckab->tcb/dot_general | solution.py:74
  251.2 6.1 %copy.39 = bf16[128,14336]{1,0:T(8,128)(2,1)} copy(bf16[128,14336]{0,1:T(8,128)(2,1)} %bitcast.17) | data formatting | bytes 7340032
  (56 shorter events, 0.6 us)
Async XLA Ops:
  7.2 114.3 %all-gather.3.cloned.1.call-start = ((), (), s32[]{:S(2)}) async-start(), calls=%async_computation | async-start | bytes 1081344 | tf_op jit(solution)/shard_map/all_gather | solution.py:64
  8.1 21.1 %collective-permute-start = (bf16[1,128,128]{2,1,0:T(8,128)(2,1)S(1)}, bf16[1,128,128]{2,1,0:T(8,128)(2,1)S(1)}, u32[]{:S(2)}, u32[]{:S(2)}) collective-permute-start(bf16[1,128,128]{2,1,0:T(8,128)(2,1)S(1)} %get-tuple-element.61), channel_id=1, source_target_pairs={{0,1},{1,2},{2,3},{3,4},{4,5},{5,6},{6,7},{7,8},{8,9},{9,10},{10,1... | collective-permute-start | bytes 98312 | tf_op jit(solution)/shard_map/ppermute | solution.py:10
  13.1 17.5 %collective-permute-start.1 = (bf16[1,128,128]{2,1,0:T(8,128)(2,1)S(1)}, bf16[1,128,128]{2,1,0:T(8,128)(2,1)S(1)}, u32[]{:S(2)}, u32[]{:S(2)}) collective-permute-start(bf16[1,128,128]{2,1,0:T(8,128)(2,1)S(1)} %get-tuple-element.61), channel_id=1, source_target_pairs={{1,0},{2,1},{3,2},{4,3},{5,4},{6,5},{7,6},{8,7},{9,8},{10,9},{11,1... | collective-permute-start | bytes 98312 | tf_op jit(solution)/shard_map/ppermute | solution.py:10
  18.2 21.5 %collective-permute-start.2 = (bf16[1,128,128]{2,1,0:T(8,128)(2,1)S(1)}, bf16[1,128,128]{2,1,0:T(8,128)(2,1)S(1)}, u32[]{:S(2)}, u32[]{:S(2)}) collective-permute-start(bf16[1,128,128]{2,1,0:T(8,128)(2,1)S(1)} %get-tuple-element.61), channel_id=1, source_target_pairs={{0,2},{1,3},{2,4},{3,5},{4,6},{5,7},{6,8},{7,9},{8,10},{9,11},{10,... | collective-permute-start | bytes 98312 | tf_op jit(solution)/shard_map/ppermute | solution.py:10
  19.5 21.6 %collective-permute-start.3 = (bf16[1,128,128]{2,1,0:T(8,128)(2,1)S(1)}, bf16[1,128,128]{2,1,0:T(8,128)(2,1)S(1)}, u32[]{:S(2)}, u32[]{:S(2)}) collective-permute-start(bf16[1,128,128]{2,1,0:T(8,128)(2,1)S(1)} %get-tuple-element.61), channel_id=1, source_target_pairs={{2,0},{3,1},{4,2},{5,3},{6,4},{7,5},{8,6},{9,7},{10,8},{11,9},{12,... | collective-permute-start | bytes 98312 | tf_op jit(solution)/shard_map/ppermute | solution.py:10
  20.8 20.3 %collective-permute-start.4 = (bf16[1,128,128]{2,1,0:T(8,128)(2,1)S(1)}, bf16[1,128,128]{2,1,0:T(8,128)(2,1)S(1)}, u32[]{:S(2)}, u32[]{:S(2)}) collective-permute-start(bf16[1,128,128]{2,1,0:T(8,128)(2,1)S(1)} %get-tuple-element.61), channel_id=1, source_target_pairs={{0,3},{1,4},{2,5},{3,6},{4,7},{5,8},{6,9},{7,10},{8,11},{9,12},{10... | collective-permute-start | bytes 98312 | tf_op jit(solution)/shard_map/ppermute | solution.py:10
  29.3 11.9 %collective-permute-start.5 = (bf16[1,128,128]{2,1,0:T(8,128)(2,1)S(1)}, bf16[1,128,128]{2,1,0:T(8,128)(2,1)S(1)}, u32[]{:S(2)}, u32[]{:S(2)}) collective-permute-start(bf16[1,128,128]{2,1,0:T(8,128)(2,1)S(1)} %get-tuple-element.61), channel_id=1, source_target_pairs={{3,0},{4,1},{5,2},{6,3},{7,4},{8,5},{9,6},{10,7},{11,8},{12,9},{13... | collective-permute-start | bytes 98312 | tf_op jit(solution)/shard_map/ppermute | solution.py:10
  30.6 10.6 %collective-permute-start.6 = (bf16[1,128,128]{2,1,0:T(8,128)(2,1)S(1)}, bf16[1,128,128]{2,1,0:T(8,128)(2,1)S(1)}, u32[]{:S(2)}, u32[]{:S(2)}) collective-permute-start(bf16[1,128,128]{2,1,0:T(8,128)(2,1)S(1)} %get-tuple-element.61), channel_id=1, source_target_pairs={{0,4},{1,5},{2,6},{3,7},{4,8},{5,9},{6,10},{7,11},{8,12},{9,13},{1... | collective-permute-start | bytes 98312 | tf_op jit(solution)/shard_map/ppermute | solution.py:10
  39.8 5.6 %collective-permute-start.7 = (bf16[1,128,128]{2,1,0:T(8,128)(2,1)S(1)}, bf16[1,128,128]{2,1,0:T(8,128)(2,1)S(1)}, u32[]{:S(2)}, u32[]{:S(2)}) collective-permute-start(bf16[1,128,128]{2,1,0:T(8,128)(2,1)S(1)} %get-tuple-element.61), channel_id=1, source_target_pairs={{4,0},{5,1},{6,2},{7,3},{8,4},{9,5},{10,6},{11,7},{12,8},{13,9},{1... | collective-permute-start | bytes 98312 | tf_op jit(solution)/shard_map/ppermute | solution.py:10
  46.6 191.1 %all-gather.5.cloned.1.call-start = ((), (), s32[]{:S(2)}) async-start(), calls=%async_computation.1 | async-start | bytes 15597568 | tf_op jit(solution)/shard_map/all_gather | solution.py:70
  125.4 32.9 %collective-permute-start.16 = (bf16[1,128,128]{2,1,0:T(8,128)(2,1)S(1)}, bf16[1,128,128]{2,1,0:T(8,128)(2,1)S(1)}, u32[]{:S(2)}, u32[]{:S(2)}) collective-permute-start(bf16[1,128,128]{2,1,0:T(8,128)(2,1)S(1)} %get-tuple-element.57), channel_id=1, source_target_pairs={{0,1},{1,2},{2,3},{3,4},{4,5},{5,6},{6,7},{7,8},{8,9},{9,10},{10,1... | collective-permute-start | bytes 98312 | tf_op jit(solution)/shard_map/ppermute | solution.py:10
  128.6 31.1 %collective-permute-start.17 = (bf16[1,128,128]{2,1,0:T(8,128)(2,1)S(1)}, bf16[1,128,128]{2,1,0:T(8,128)(2,1)S(1)}, u32[]{:S(2)}, u32[]{:S(2)}) collective-permute-start(bf16[1,128,128]{2,1,0:T(8,128)(2,1)S(1)} %get-tuple-element.57), channel_id=1, source_target_pairs={{1,0},{2,1},{3,2},{4,3},{5,4},{6,5},{7,6},{8,7},{9,8},{10,9},{11,1... | collective-permute-start | bytes 98312 | tf_op jit(solution)/shard_map/ppermute | solution.py:10
  130.5 35.8 %collective-permute-start.18 = (bf16[1,128,128]{2,1,0:T(8,128)(2,1)S(1)}, bf16[1,128,128]{2,1,0:T(8,128)(2,1)S(1)}, u32[]{:S(2)}, u32[]{:S(2)}) collective-permute-start(bf16[1,128,128]{2,1,0:T(8,128)(2,1)S(1)} %get-tuple-element.57), channel_id=1, source_target_pairs={{0,2},{1,3},{2,4},{3,5},{4,6},{5,7},{6,8},{7,9},{8,10},{9,11},{10,... | collective-permute-start | bytes 98312 | tf_op jit(solution)/shard_map/ppermute | solution.py:10
  132.8 34.8 %collective-permute-start.19 = (bf16[1,128,128]{2,1,0:T(8,128)(2,1)S(1)}, bf16[1,128,128]{2,1,0:T(8,128)(2,1)S(1)}, u32[]{:S(2)}, u32[]{:S(2)}) collective-permute-start(bf16[1,128,128]{2,1,0:T(8,128)(2,1)S(1)} %get-tuple-element.57), channel_id=1, source_target_pairs={{2,0},{3,1},{4,2},{5,3},{6,4},{7,5},{8,6},{9,7},{10,8},{11,9},{12,... | collective-permute-start | bytes 98312 | tf_op jit(solution)/shard_map/ppermute | solution.py:10
  134.1 35.7 %collective-permute-start.20 = (bf16[1,128,128]{2,1,0:T(8,128)(2,1)S(1)}, bf16[1,128,128]{2,1,0:T(8,128)(2,1)S(1)}, u32[]{:S(2)}, u32[]{:S(2)}) collective-permute-start(bf16[1,128,128]{2,1,0:T(8,128)(2,1)S(1)} %get-tuple-element.57), channel_id=1, source_target_pairs={{0,3},{1,4},{2,5},{3,6},{4,7},{5,8},{6,9},{7,10},{8,11},{9,12},{10... | collective-permute-start | bytes 98312 | tf_op jit(solution)/shard_map/ppermute | solution.py:10
  158.4 13.7 %collective-permute-start.21 = (bf16[1,128,128]{2,1,0:T(8,128)(2,1)S(1)}, bf16[1,128,128]{2,1,0:T(8,128)(2,1)S(1)}, u32[]{:S(2)}, u32[]{:S(2)}) collective-permute-start(bf16[1,128,128]{2,1,0:T(8,128)(2,1)S(1)} %get-tuple-element.57), channel_id=1, source_target_pairs={{3,0},{4,1},{5,2},{6,3},{7,4},{8,5},{9,6},{10,7},{11,8},{12,9},{13... | collective-permute-start | bytes 98312 | tf_op jit(solution)/shard_map/ppermute | solution.py:10
  159.7 18.8 %collective-permute-start.22 = (bf16[1,128,128]{2,1,0:T(8,128)(2,1)S(1)}, bf16[1,128,128]{2,1,0:T(8,128)(2,1)S(1)}, u32[]{:S(2)}, u32[]{:S(2)}) collective-permute-start(bf16[1,128,128]{2,1,0:T(8,128)(2,1)S(1)} %get-tuple-element.57), channel_id=1, source_target_pairs={{0,4},{1,5},{2,6},{3,7},{4,8},{5,9},{6,10},{7,11},{8,12},{9,13},{1... | collective-permute-start | bytes 98312 | tf_op jit(solution)/shard_map/ppermute | solution.py:10
  166.3 13.5 %collective-permute-start.23 = (bf16[1,128,128]{2,1,0:T(8,128)(2,1)S(1)}, bf16[1,128,128]{2,1,0:T(8,128)(2,1)S(1)}, u32[]{:S(2)}, u32[]{:S(2)}) collective-permute-start(bf16[1,128,128]{2,1,0:T(8,128)(2,1)S(1)} %get-tuple-element.57), channel_id=1, source_target_pairs={{4,0},{5,1},{6,2},{7,3},{8,4},{9,5},{10,6},{11,7},{12,8},{13,9},{1... | collective-permute-start | bytes 98312 | tf_op jit(solution)/shard_map/ppermute | solution.py:10
  167.6 18.2 %collective-permute-start.8 = (bf16[1,128,128]{2,1,0:T(8,128)(2,1)S(1)}, bf16[1,128,128]{2,1,0:T(8,128)(2,1)S(1)}, u32[]{:S(2)}, u32[]{:S(2)}) collective-permute-start(bf16[1,128,128]{2,1,0:T(8,128)(2,1)S(1)} %get-tuple-element.59), channel_id=1, source_target_pairs={{0,1},{1,2},{2,3},{3,4},{4,5},{5,6},{6,7},{7,8},{8,9},{9,10},{10,1... | collective-permute-start | bytes 98312 | tf_op jit(solution)/shard_map/ppermute | solution.py:10
  169.8 17.3 %collective-permute-start.9 = (bf16[1,128,128]{2,1,0:T(8,128)(2,1)S(1)}, bf16[1,128,128]{2,1,0:T(8,128)(2,1)S(1)}, u32[]{:S(2)}, u32[]{:S(2)}) collective-permute-start(bf16[1,128,128]{2,1,0:T(8,128)(2,1)S(1)} %get-tuple-element.59), channel_id=1, source_target_pairs={{1,0},{2,1},{3,2},{4,3},{5,4},{6,5},{7,6},{8,7},{9,8},{10,9},{11,1... | collective-permute-start | bytes 98312 | tf_op jit(solution)/shard_map/ppermute | solution.py:10
  172.0 24.0 %collective-permute-start.10 = (bf16[1,128,128]{2,1,0:T(8,128)(2,1)S(1)}, bf16[1,128,128]{2,1,0:T(8,128)(2,1)S(1)}, u32[]{:S(2)}, u32[]{:S(2)}) collective-permute-start(bf16[1,128,128]{2,1,0:T(8,128)(2,1)S(1)} %get-tuple-element.59), channel_id=1, source_target_pairs={{0,2},{1,3},{2,4},{3,5},{4,6},{5,7},{6,8},{7,9},{8,10},{9,11},{10,... | collective-permute-start | bytes 98312 | tf_op jit(solution)/shard_map/ppermute | solution.py:10
  178.5 18.8 %collective-permute-start.11 = (bf16[1,128,128]{2,1,0:T(8,128)(2,1)S(1)}, bf16[1,128,128]{2,1,0:T(8,128)(2,1)S(1)}, u32[]{:S(2)}, u32[]{:S(2)}) collective-permute-start(bf16[1,128,128]{2,1,0:T(8,128)(2,1)S(1)} %get-tuple-element.59), channel_id=1, source_target_pairs={{2,0},{3,1},{4,2},{5,3},{6,4},{7,5},{8,6},{9,7},{10,8},{11,9},{12,... | collective-permute-start | bytes 98312 | tf_op jit(solution)/shard_map/ppermute | solution.py:10
  179.8 17.5 %collective-permute-start.12 = (bf16[1,128,128]{2,1,0:T(8,128)(2,1)S(1)}, bf16[1,128,128]{2,1,0:T(8,128)(2,1)S(1)}, u32[]{:S(2)}, u32[]{:S(2)}) collective-permute-start(bf16[1,128,128]{2,1,0:T(8,128)(2,1)S(1)} %get-tuple-element.59), channel_id=1, source_target_pairs={{0,3},{1,4},{2,5},{3,6},{4,7},{5,8},{6,9},{7,10},{8,11},{9,12},{10... | collective-permute-start | bytes 98312 | tf_op jit(solution)/shard_map/ppermute | solution.py:10
  185.9 11.5 %collective-permute-start.13 = (bf16[1,128,128]{2,1,0:T(8,128)(2,1)S(1)}, bf16[1,128,128]{2,1,0:T(8,128)(2,1)S(1)}, u32[]{:S(2)}, u32[]{:S(2)}) collective-permute-start(bf16[1,128,128]{2,1,0:T(8,128)(2,1)S(1)} %get-tuple-element.59), channel_id=1, source_target_pairs={{3,0},{4,1},{5,2},{6,3},{7,4},{8,5},{9,6},{10,7},{11,8},{12,9},{13... | collective-permute-start | bytes 98312 | tf_op jit(solution)/shard_map/ppermute | solution.py:10
  187.2 10.2 %collective-permute-start.14 = (bf16[1,128,128]{2,1,0:T(8,128)(2,1)S(1)}, bf16[1,128,128]{2,1,0:T(8,128)(2,1)S(1)}, u32[]{:S(2)}, u32[]{:S(2)}) collective-permute-start(bf16[1,128,128]{2,1,0:T(8,128)(2,1)S(1)} %get-tuple-element.59), channel_id=1, source_target_pairs={{0,4},{1,5},{2,6},{3,7},{4,8},{5,9},{6,10},{7,11},{8,12},{9,13},{1... | collective-permute-start | bytes 98312 | tf_op jit(solution)/shard_map/ppermute | solution.py:10
  196.0 6.0 %collective-permute-start.15 = (bf16[1,128,128]{2,1,0:T(8,128)(2,1)S(1)}, bf16[1,128,128]{2,1,0:T(8,128)(2,1)S(1)}, u32[]{:S(2)}, u32[]{:S(2)}) collective-permute-start(bf16[1,128,128]{2,1,0:T(8,128)(2,1)S(1)} %get-tuple-element.59), channel_id=1, source_target_pairs={{4,0},{5,1},{6,2},{7,3},{8,4},{9,5},{10,6},{11,7},{12,8},{13,9},{1... | collective-permute-start | bytes 98312 | tf_op jit(solution)/shard_map/ppermute | solution.py:10
Sparse Core Ops, SparseCore 0:
  46.8 74.6 all-gather.2
  125.1 112.6 all-gather.4
where the time goes:
time: 265 us; the launch traced here: 264 us
  waiting for transfers between devices  116 us (44%)
  starting transfers between devices  82.8 us (31%)
  local copies, waits for them, and re-layouts  25.5 us (10%)
  between operations  15.3 us (6%)
  matrix products  13.5 us (5%)
  other arithmetic  11.3 us (4%)
    ppermute x24, starting transfers between devices, passed_along(): return lax.ppermute(block, axis, route)  82.7 us
    all_gather x1, waiting for transfers between devices, on_device(): group_cells = lax.all_gather(cell_blocks, 'dp', axis=0, tiled=True)  73.8 us
    all_gather x1, waiting for transfers between devices, on_device(): panel_piece = lax.all_gather(panel, 'fsdp', axis=0, tiled=True)  34.5 us
    dot_general x1, matrix products, on_device(): jnp.einsum('tcka,ckab->tcb', picked, panel_piece, preferred_element_type=...  13.5 us
    gather x1, local copies, waits for them, and re-layouts, on_device(): picked = jnp.take(token_blocks, new_rows.reshape(-1), axis=1)  13.3 us
    unnamed x4, local copies, waits for them, and re-layouts  9.25 us
    ppermute x24, waiting for transfers between devices, passed_along(): return lax.ppermute(block, axis, route)  7.47 us
  transfers between devices with their start and end apart: 26, of which 4 were waited for; matrix products, arithmetic and copies ran while one was open for 10% of the time, Pallas kernels for 0%

commit v1 on v0

--- a/solution.py
+++ b/solution.py
@@ -2,6 +2,7 @@
 import jax.numpy as jnp
 from jax import lax
 from jax.sharding import PartitionSpec as P
+from jax.lax import all_to_all, axis_size
 
 
 def passed_along(block, axis, distance):
@@ -61,7 +62,15 @@
     moment_new = settle(1)
     second_new = settle(2)
     cell_blocks = master_new.astype(jnp.bfloat16)
-    group_cells = lax.all_gather(cell_blocks, "dp", axis=0, tiled=True)
+    group_cells = jnp.concatenate(
+        all_to_all(
+            jnp.stack([cell_blocks] * axis_size("dp"), axis=0),
+            axis_name="dp",
+            split_axis=0,
+            concat_axis=0,
+        ),
+        axis=0,
+    )
     panel = jnp.take(group_cells, new_flat, axis=0).reshape(
         column_count, nonzero_count, block_size, block_size
     )

time: 265 us -> 256 us (0.966)
  waiting for transfers between devices: 116 us -> 95.4 us
  starting transfers between devices: 82.8 us -> 93.6 us
    all_gather x1 -> x0, waiting for transfers between devices: 73.8 us -> none  [on_device(): group_cells = lax.all_gather(cell_blocks, 'dp', axis=0, tiled=True)]
    all_to_all x0 -> x1, waiting for transfers between devices: none -> 54.7 us  [on_device(): all_to_all(jnp.stack([cell_blocks] * axis_size('dp'), axis=0), axis_name=...]
    all_to_all x0 -> x1, starting transfers between devices: none -> 15 us  [on_device(): all_to_all(jnp.stack([cell_blocks] * axis_size('dp'), axis=0), axis_name=...]
    ppermute x24, starting transfers between devices: 82.7 us -> 78.6 us  [passed_along(): return lax.ppermute(block, axis, route)]
where the time goes in v1:
time: 256 us; the launch traced here: 254 us
  waiting for transfers between devices  95.4 us (37%)
  starting transfers between devices  93.6 us (37%)
  local copies, waits for them, and re-layouts  25.5 us (10%)
  between operations  15.3 us (6%)
  matrix products  13.5 us (5%)
  other arithmetic  11.1 us (4%)
    ppermute x24, starting transfers between devices, passed_along(): return lax.ppermute(block, axis, route)  78.6 us
    all_to_all x1, waiting for transfers between devices, on_device(): all_to_all(jnp.stack([cell_blocks] * axis_size('dp'), axis=0), axis_name=...  54.7 us
    all_gather x1, waiting for transfers between devices, on_device(): panel_piece = lax.all_gather(panel, 'fsdp', axis=0, tiled=True)  33.1 us
    all_to_all x1, starting transfers between devices, on_device(): all_to_all(jnp.stack([cell_blocks] * axis_size('dp'), axis=0), axis_name=...  15 us
    dot_general x1, matrix products, on_device(): jnp.einsum('tcka,ckab->tcb', picked, panel_piece, preferred_element_type=...  13.5 us
    gather x1, local copies, waits for them, and re-layouts, on_device(): picked = jnp.take(token_blocks, new_rows.reshape(-1), axis=1)  13.3 us
    unnamed x4, local copies, waits for them, and re-layouts  9.25 us
    ppermute x24, waiting for transfers between devices, passed_along(): return lax.ppermute(block, axis, route)  7.52 us
  transfers between devices with their start and end apart: 26, of which 4 were waited for; matrix products, arithmetic and copies ran while one was open for 10% of the time, Pallas kernels for 0%

profile of v1, /device:TPU:1, one launch (start us, length us, event | category | flops | bytes accessed | tf_op | source)
XLA Modules:
  0.0 254.3 jit_solution(15302428616678011010)
XLA Ops:
  7.2 0.9 fusion.10
  8.1 4.9 %collective-permute-start = (bf16[1,128,128]{2,1,0:T(8,128)(2,1)S(1)}, bf16[1,128,128]{2,1,0:T(8,128)(2,1)S(1)}, u32[]{:S(2)}, u32[]{:S(2)}) collective-permute-start(bf16[1,128,128]{2,1,0:T(8,128)(2,1)S(1)} %get-tuple-element.61), channel_id=1, source_target_pairs={{0,1},{1,2},{2,3},{3,4},{4,5},{5,6},{6,7},{7,8},{8,9},{9,10},{10,1... | collective-permute-start | bytes 98312 | tf_op jit(solution)/shard_map/ppermute | solution.py:11
  13.0 5.1 %collective-permute-start.1 = (bf16[1,128,128]{2,1,0:T(8,128)(2,1)S(1)}, bf16[1,128,128]{2,1,0:T(8,128)(2,1)S(1)}, u32[]{:S(2)}, u32[]{:S(2)}) collective-permute-start(bf16[1,128,128]{2,1,0:T(8,128)(2,1)S(1)} %get-tuple-element.61), channel_id=1, source_target_pairs={{1,0},{2,1},{3,2},{4,3},{5,4},{6,5},{7,6},{8,7},{9,8},{10,9},{11,1... | collective-permute-start | bytes 98312 | tf_op jit(solution)/shard_map/ppermute | solution.py:11
  18.2 1.3 collective-permute-start.2
  19.5 1.3 collective-permute-start.3
  20.8 5.0 %collective-permute-start.4 = (bf16[1,128,128]{2,1,0:T(8,128)(2,1)S(1)}, bf16[1,128,128]{2,1,0:T(8,128)(2,1)S(1)}, u32[]{:S(2)}, u32[]{:S(2)}) collective-permute-start(bf16[1,128,128]{2,1,0:T(8,128)(2,1)S(1)} %get-tuple-element.61), channel_id=1, source_target_pairs={{0,3},{1,4},{2,5},{3,6},{4,7},{5,8},{6,9},{7,10},{8,11},{9,12},{10... | collective-permute-start | bytes 98312 | tf_op jit(solution)/shard_map/ppermute | solution.py:11
  25.8 1.3 and_reduce_fusion
  27.2 1.3 select_reduce_fusion
  29.2 1.3 collective-permute-start.5
  30.5 9.2 %collective-permute-start.6 = (bf16[1,128,128]{2,1,0:T(8,128)(2,1)S(1)}, bf16[1,128,128]{2,1,0:T(8,128)(2,1)S(1)}, u32[]{:S(2)}, u32[]{:S(2)}) collective-permute-start(bf16[1,128,128]{2,1,0:T(8,128)(2,1)S(1)} %get-tuple-element.61), channel_id=1, source_target_pairs={{0,4},{1,5},{2,6},{3,7},{4,8},{5,9},{6,10},{7,11},{8,12},{9,13},{1... | collective-permute-start | bytes 98312 | tf_op jit(solution)/shard_map/ppermute | solution.py:11
  39.7 1.3 collective-permute-start.7
  41.1 4.1 %collective-permute-done.7 = bf16[1,128,128]{2,1,0:T(8,128)(2,1)S(1)} collective-permute-done((bf16[1,128,128]{2,1,0:T(8,128)(2,1)S(1)}, bf16[1,128,128]{2,1,0:T(8,128)(2,1)S(1)}, u32[]{:S(2)}, u32[]{:S(2)}) %collective-permute-start.7) | collective-permute-done | bytes 32800 | tf_op jit(solution)/shard_map/ppermute | solution.py:11
  45.3 1.2 convert_bitcast_fusion
  46.5 1.2 stack.2
  47.7 15.0 %all-to-all-start = ((bf16[32,1,128,128]{3,2,1,0:T(8,128)(2,1)}), bf16[32,1,128,128]{3,2,1,0:T(8,128)(2,1)S(1)}, u32[]{:S(2)}, u32[]{:S(2)}) async-start(bf16[32,1,128,128]{3,2,1,0:T(8,128)(2,1)} %stack.2), calls=%async_computation | async-start | bytes 2097152 | tf_op jit(solution)/shard_map/all_to_all | solution.py:66
  62.7 0.8 copy.32
  63.7 54.7 %all-to-all-done = bf16[32,1,128,128]{3,2,1,0:T(8,128)(2,1)S(1)} async-done(((bf16[32,1,128,128]{3,2,1,0:T(8,128)(2,1)}), bf16[32,1,128,128]{3,2,1,0:T(8,128)(2,1)S(1)}, u32[]{:S(2)}, u32[]{:S(2)}) %all-to-all-start) | async-done | bytes 1048608 | tf_op jit(solution)/shard_map/all_to_all | solution.py:66
  118.4 0.7 gather_fusion
  119.1 1.1 broadcast_select_fusion
  120.2 0.9 fusion.8
  121.1 1.9 collective-permute-start.16
  123.1 2.4 collective-permute-start.17
  125.5 1.5 collective-permute-start.18
  127.0 1.3 collective-permute-start.19
  128.3 5.6 %collective-permute-start.20 = (bf16[1,128,128]{2,1,0:T(8,128)(2,1)S(1)}, bf16[1,128,128]{2,1,0:T(8,128)(2,1)S(1)}, u32[]{:S(2)}, u32[]{:S(2)}) collective-permute-start(bf16[1,128,128]{2,1,0:T(8,128)(2,1)S(1)} %get-tuple-element.57), channel_id=1, source_target_pairs={{0,3},{1,4},{2,5},{3,6},{4,7},{5,8},{6,9},{7,10},{8,11},{9,12},{10... | collective-permute-start | bytes 98312 | tf_op jit(solution)/shard_map/ppermute | solution.py:11
  133.9 0.8 copy.35
  134.8 0.7 compare_and_fusion
  135.5 0.9 fusion.9
  136.5 1.6 copy.34
  138.1 0.7 copy.36
  138.9 13.3 %gather_fusion.1 = bf16[448,128,128]{2,1,0:T(8,128)(2,1)} fusion(bf16[128,32,128]{2,0,1:T(8,128)(2,1)S(1)} %copy.36, s32[1024]{0:T(1024)S(1)} %pad_clamp_fusion), kind=kCustom, calls=%fused_computation.1 | custom fusion | bytes 29361920 | tf_op jit(solution)/shard_map/jit(_take)/gather | solution.py:81
  152.2 1.3 collective-permute-start.21
  153.5 4.3 %collective-permute-start.22 = (bf16[1,128,128]{2,1,0:T(8,128)(2,1)S(1)}, bf16[1,128,128]{2,1,0:T(8,128)(2,1)S(1)}, u32[]{:S(2)}, u32[]{:S(2)}) collective-permute-start(bf16[1,128,128]{2,1,0:T(8,128)(2,1)S(1)} %get-tuple-element.57), channel_id=1, source_target_pairs={{0,4},{1,5},{2,6},{3,7},{4,8},{5,9},{6,10},{7,11},{8,12},{9,13},{1... | collective-permute-start | bytes 98312 | tf_op jit(solution)/shard_map/ppermute | solution.py:11
  157.8 1.3 collective-permute-start.23
  159.2 3.6 %collective-permute-start.8 = (bf16[1,128,128]{2,1,0:T(8,128)(2,1)S(1)}, bf16[1,128,128]{2,1,0:T(8,128)(2,1)S(1)}, u32[]{:S(2)}, u32[]{:S(2)}) collective-permute-start(bf16[1,128,128]{2,1,0:T(8,128)(2,1)S(1)} %get-tuple-element.59), channel_id=1, source_target_pairs={{0,1},{1,2},{2,3},{3,4},{4,5},{5,6},{6,7},{7,8},{8,9},{9,10},{10,1... | collective-permute-start | bytes 98312 | tf_op jit(solution)/shard_map/ppermute | solution.py:11
  162.8 1.9 collective-permute-start.9
  164.7 5.3 %collective-permute-start.10 = (bf16[1,128,128]{2,1,0:T(8,128)(2,1)S(1)}, bf16[1,128,128]{2,1,0:T(8,128)(2,1)S(1)}, u32[]{:S(2)}, u32[]{:S(2)}) collective-permute-start(bf16[1,128,128]{2,1,0:T(8,128)(2,1)S(1)} %get-tuple-element.59), channel_id=1, source_target_pairs={{0,2},{1,3},{2,4},{3,5},{4,6},{5,7},{6,8},{7,9},{8,10},{9,11},{10,... | collective-permute-start | bytes 98312 | tf_op jit(solution)/shard_map/ppermute | solution.py:11
  170.1 1.3 collective-permute-start.11
  171.4 6.0 %collective-permute-start.12 = (bf16[1,128,128]{2,1,0:T(8,128)(2,1)S(1)}, bf16[1,128,128]{2,1,0:T(8,128)(2,1)S(1)}, u32[]{:S(2)}, u32[]{:S(2)}) collective-permute-start(bf16[1,128,128]{2,1,0:T(8,128)(2,1)S(1)} %get-tuple-element.59), channel_id=1, source_target_pairs={{0,3},{1,4},{2,5},{3,6},{4,7},{5,8},{6,9},{7,10},{8,11},{9,12},{10... | collective-permute-start | bytes 98312 | tf_op jit(solution)/shard_map/ppermute | solution.py:11
  177.4 1.3 collective-permute-start.13
  178.7 8.8 %collective-permute-start.14 = (bf16[1,128,128]{2,1,0:T(8,128)(2,1)S(1)}, bf16[1,128,128]{2,1,0:T(8,128)(2,1)S(1)}, u32[]{:S(2)}, u32[]{:S(2)}) collective-permute-start(bf16[1,128,128]{2,1,0:T(8,128)(2,1)S(1)} %get-tuple-element.59), channel_id=1, source_target_pairs={{0,4},{1,5},{2,6},{3,7},{4,8},{5,9},{6,10},{7,11},{8,12},{9,13},{1... | collective-permute-start | bytes 98312 | tf_op jit(solution)/shard_map/ppermute | solution.py:11
  187.6 1.3 collective-permute-start.15
  189.0 1.2 dynamic-slice_select_fusion
  190.2 3.3 %collective-permute-done.15 = bf16[1,128,128]{2,1,0:T(8,128)(2,1)S(1)} collective-permute-done((bf16[1,128,128]{2,1,0:T(8,128)(2,1)S(1)}, bf16[1,128,128]{2,1,0:T(8,128)(2,1)S(1)}, u32[]{:S(2)}, u32[]{:S(2)}) %collective-permute-start.15) | collective-permute-done | bytes 32800 | tf_op jit(solution)/shard_map/ppermute | solution.py:11
  193.5 1.2 dynamic-slice_select_fusion.1
  194.7 33.1 %all-gather.2.cloned.1.call-done = bf16[112,4,128,128]{3,2,1,0:T(8,128)(2,1)} async-done(((bf16[7,4,128,128]{3,2,1,0:T(8,128)(2,1)}), bf16[112,4,128,128]{3,2,1,0:T(8,128)(2,1)}) %all-gather.2.cloned.1.call-update) | async-done | bytes 14680080 | tf_op jit(solution)/shard_map/all_gather | solution.py:79
  227.9 13.5 %bitcast_convert_fusion = bf16[112,128,128]{2,1,0:T(8,128)(2,1)} fusion(bf16[112,4,128,128]{3,2,1,0:T(8,128)(2,1)} %all-gather.2.cloned.1.call-done, bf16[128,112,4,128]{3,0,2,1:T(8,128)(2,1)} %bitcast.18, pred[112,4]{1,0:T(8,128)(4,1)S(1)} %copy.33), kind=kOutput, calls=%fused_computation.5 | convolution fusion | flops 1888223232 | bytes 33030592 | tf_op jit(solution)/shard_map/tcka,ckab->tcb/dot_general | solution.py:83
  241.3 6.1 %copy.38 = bf16[128,14336]{1,0:T(8,128)(2,1)} copy(bf16[128,14336]{0,1:T(8,128)(2,1)} %bitcast.21) | data formatting | bytes 7340032
  (56 shorter events, 0.7 us)
Async XLA Ops:
  8.1 21.1 %collective-permute-start = (bf16[1,128,128]{2,1,0:T(8,128)(2,1)S(1)}, bf16[1,128,128]{2,1,0:T(8,128)(2,1)S(1)}, u32[]{:S(2)}, u32[]{:S(2)}) collective-permute-start(bf16[1,128,128]{2,1,0:T(8,128)(2,1)S(1)} %get-tuple-element.61), channel_id=1, source_target_pairs={{0,1},{1,2},{2,3},{3,4},{4,5},{5,6},{6,7},{7,8},{8,9},{9,10},{10,1... | collective-permute-start | bytes 98312 | tf_op jit(solution)/shard_map/ppermute | solution.py:11
  13.0 17.4 %collective-permute-start.1 = (bf16[1,128,128]{2,1,0:T(8,128)(2,1)S(1)}, bf16[1,128,128]{2,1,0:T(8,128)(2,1)S(1)}, u32[]{:S(2)}, u32[]{:S(2)}) collective-permute-start(bf16[1,128,128]{2,1,0:T(8,128)(2,1)S(1)} %get-tuple-element.61), channel_id=1, source_target_pairs={{1,0},{2,1},{3,2},{4,3},{5,4},{6,5},{7,6},{8,7},{9,8},{10,9},{11,1... | collective-permute-start | bytes 98312 | tf_op jit(solution)/shard_map/ppermute | solution.py:11
  18.2 21.5 %collective-permute-start.2 = (bf16[1,128,128]{2,1,0:T(8,128)(2,1)S(1)}, bf16[1,128,128]{2,1,0:T(8,128)(2,1)S(1)}, u32[]{:S(2)}, u32[]{:S(2)}) collective-permute-start(bf16[1,128,128]{2,1,0:T(8,128)(2,1)S(1)} %get-tuple-element.61), channel_id=1, source_target_pairs={{0,2},{1,3},{2,4},{3,5},{4,6},{5,7},{6,8},{7,9},{8,10},{9,11},{10,... | collective-permute-start | bytes 98312 | tf_op jit(solution)/shard_map/ppermute | solution.py:11
  19.5 21.5 %collective-permute-start.3 = (bf16[1,128,128]{2,1,0:T(8,128)(2,1)S(1)}, bf16[1,128,128]{2,1,0:T(8,128)(2,1)S(1)}, u32[]{:S(2)}, u32[]{:S(2)}) collective-permute-start(bf16[1,128,128]{2,1,0:T(8,128)(2,1)S(1)} %get-tuple-element.61), channel_id=1, source_target_pairs={{2,0},{3,1},{4,2},{5,3},{6,4},{7,5},{8,6},{9,7},{10,8},{11,9},{12,... | collective-permute-start | bytes 98312 | tf_op jit(solution)/shard_map/ppermute | solution.py:11
  20.8 20.2 %collective-permute-start.4 = (bf16[1,128,128]{2,1,0:T(8,128)(2,1)S(1)}, bf16[1,128,128]{2,1,0:T(8,128)(2,1)S(1)}, u32[]{:S(2)}, u32[]{:S(2)}) collective-permute-start(bf16[1,128,128]{2,1,0:T(8,128)(2,1)S(1)} %get-tuple-element.61), channel_id=1, source_target_pairs={{0,3},{1,4},{2,5},{3,6},{4,7},{5,8},{6,9},{7,10},{8,11},{9,12},{10... | collective-permute-start | bytes 98312 | tf_op jit(solution)/shard_map/ppermute | solution.py:11
  29.2 11.9 %collective-permute-start.5 = (bf16[1,128,128]{2,1,0:T(8,128)(2,1)S(1)}, bf16[1,128,128]{2,1,0:T(8,128)(2,1)S(1)}, u32[]{:S(2)}, u32[]{:S(2)}) collective-permute-start(bf16[1,128,128]{2,1,0:T(8,128)(2,1)S(1)} %get-tuple-element.61), channel_id=1, source_target_pairs={{3,0},{4,1},{5,2},{6,3},{7,4},{8,5},{9,6},{10,7},{11,8},{12,9},{13... | collective-permute-start | bytes 98312 | tf_op jit(solution)/shard_map/ppermute | solution.py:11
  30.5 10.6 %collective-permute-start.6 = (bf16[1,128,128]{2,1,0:T(8,128)(2,1)S(1)}, bf16[1,128,128]{2,1,0:T(8,128)(2,1)S(1)}, u32[]{:S(2)}, u32[]{:S(2)}) collective-permute-start(bf16[1,128,128]{2,1,0:T(8,128)(2,1)S(1)} %get-tuple-element.61), channel_id=1, source_target_pairs={{0,4},{1,5},{2,6},{3,7},{4,8},{5,9},{6,10},{7,11},{8,12},{9,13},{1... | collective-permute-start | bytes 98312 | tf_op jit(solution)/shard_map/ppermute | solution.py:11
  39.7 5.6 %collective-permute-start.7 = (bf16[1,128,128]{2,1,0:T(8,128)(2,1)S(1)}, bf16[1,128,128]{2,1,0:T(8,128)(2,1)S(1)}, u32[]{:S(2)}, u32[]{:S(2)}) collective-permute-start(bf16[1,128,128]{2,1,0:T(8,128)(2,1)S(1)} %get-tuple-element.61), channel_id=1, source_target_pairs={{4,0},{5,1},{6,2},{7,3},{8,4},{9,5},{10,6},{11,7},{12,8},{13,9},{1... | collective-permute-start | bytes 98312 | tf_op jit(solution)/shard_map/ppermute | solution.py:11
  47.7 70.7 %all-to-all-start = ((bf16[32,1,128,128]{3,2,1,0:T(8,128)(2,1)}), bf16[32,1,128,128]{3,2,1,0:T(8,128)(2,1)S(1)}, u32[]{:S(2)}, u32[]{:S(2)}) async-start(bf16[32,1,128,128]{3,2,1,0:T(8,128)(2,1)} %stack.2), calls=%async_computation | async-start | bytes 2097152 | tf_op jit(solution)/shard_map/all_to_all | solution.py:66
  62.6 165.2 %all-gather.2.cloned.1.call-start = ((), (), s32[]{:S(2)}) async-start(), calls=%async_computation.1 | async-start | bytes 15597568 | tf_op jit(solution)/shard_map/all_gather | solution.py:79
  121.1 31.1 %collective-permute-start.16 = (bf16[1,128,128]{2,1,0:T(8,128)(2,1)S(1)}, bf16[1,128,128]{2,1,0:T(8,128)(2,1)S(1)}, u32[]{:S(2)}, u32[]{:S(2)}) collective-permute-start(bf16[1,128,128]{2,1,0:T(8,128)(2,1)S(1)} %get-tuple-element.57), channel_id=1, source_target_pairs={{0,1},{1,2},{2,3},{3,4},{4,5},{5,6},{6,7},{7,8},{8,9},{9,10},{10,1... | collective-permute-start | bytes 98312 | tf_op jit(solution)/shard_map/ppermute | solution.py:11
  123.1 30.4 %collective-permute-start.17 = (bf16[1,128,128]{2,1,0:T(8,128)(2,1)S(1)}, bf16[1,128,128]{2,1,0:T(8,128)(2,1)S(1)}, u32[]{:S(2)}, u32[]{:S(2)}) collective-permute-start(bf16[1,128,128]{2,1,0:T(8,128)(2,1)S(1)} %get-tuple-element.57), channel_id=1, source_target_pairs={{1,0},{2,1},{3,2},{4,3},{5,4},{6,5},{7,6},{8,7},{9,8},{10,9},{11,1... | collective-permute-start | bytes 98312 | tf_op jit(solution)/shard_map/ppermute | solution.py:11
  125.5 32.4 %collective-permute-start.18 = (bf16[1,128,128]{2,1,0:T(8,128)(2,1)S(1)}, bf16[1,128,128]{2,1,0:T(8,128)(2,1)S(1)}, u32[]{:S(2)}, u32[]{:S(2)}) collective-permute-start(bf16[1,128,128]{2,1,0:T(8,128)(2,1)S(1)} %get-tuple-element.57), channel_id=1, source_target_pairs={{0,2},{1,3},{2,4},{3,5},{4,6},{5,7},{6,8},{7,9},{8,10},{9,11},{10,... | collective-permute-start | bytes 98312 | tf_op jit(solution)/shard_map/ppermute | solution.py:11
  127.0 32.2 %collective-permute-start.19 = (bf16[1,128,128]{2,1,0:T(8,128)(2,1)S(1)}, bf16[1,128,128]{2,1,0:T(8,128)(2,1)S(1)}, u32[]{:S(2)}, u32[]{:S(2)}) collective-permute-start(bf16[1,128,128]{2,1,0:T(8,128)(2,1)S(1)} %get-tuple-element.57), channel_id=1, source_target_pairs={{2,0},{3,1},{4,2},{5,3},{6,4},{7,5},{8,6},{9,7},{10,8},{11,9},{12,... | collective-permute-start | bytes 98312 | tf_op jit(solution)/shard_map/ppermute | solution.py:11
  128.3 34.5 %collective-permute-start.20 = (bf16[1,128,128]{2,1,0:T(8,128)(2,1)S(1)}, bf16[1,128,128]{2,1,0:T(8,128)(2,1)S(1)}, u32[]{:S(2)}, u32[]{:S(2)}) collective-permute-start(bf16[1,128,128]{2,1,0:T(8,128)(2,1)S(1)} %get-tuple-element.57), channel_id=1, source_target_pairs={{0,3},{1,4},{2,5},{3,6},{4,7},{5,8},{6,9},{7,10},{8,11},{9,12},{10... | collective-permute-start | bytes 98312 | tf_op jit(solution)/shard_map/ppermute | solution.py:11
  152.2 12.5 %collective-permute-start.21 = (bf16[1,128,128]{2,1,0:T(8,128)(2,1)S(1)}, bf16[1,128,128]{2,1,0:T(8,128)(2,1)S(1)}, u32[]{:S(2)}, u32[]{:S(2)}) collective-permute-start(bf16[1,128,128]{2,1,0:T(8,128)(2,1)S(1)} %get-tuple-element.57), channel_id=1, source_target_pairs={{3,0},{4,1},{5,2},{6,3},{7,4},{8,5},{9,6},{10,7},{11,8},{12,9},{13... | collective-permute-start | bytes 98312 | tf_op jit(solution)/shard_map/ppermute | solution.py:11
  153.5 16.6 %collective-permute-start.22 = (bf16[1,128,128]{2,1,0:T(8,128)(2,1)S(1)}, bf16[1,128,128]{2,1,0:T(8,128)(2,1)S(1)}, u32[]{:S(2)}, u32[]{:S(2)}) collective-permute-start(bf16[1,128,128]{2,1,0:T(8,128)(2,1)S(1)} %get-tuple-element.57), channel_id=1, source_target_pairs={{0,4},{1,5},{2,6},{3,7},{4,8},{5,9},{6,10},{7,11},{8,12},{9,13},{1... | collective-permute-start | bytes 98312 | tf_op jit(solution)/shard_map/ppermute | solution.py:11
  157.8 13.5 %collective-permute-start.23 = (bf16[1,128,128]{2,1,0:T(8,128)(2,1)S(1)}, bf16[1,128,128]{2,1,0:T(8,128)(2,1)S(1)}, u32[]{:S(2)}, u32[]{:S(2)}) collective-permute-start(bf16[1,128,128]{2,1,0:T(8,128)(2,1)S(1)} %get-tuple-element.57), channel_id=1, source_target_pairs={{4,0},{5,1},{6,2},{7,3},{8,4},{9,5},{10,6},{11,7},{12,8},{13,9},{1... | collective-permute-start | bytes 98312 | tf_op jit(solution)/shard_map/ppermute | solution.py:11
  159.2 18.2 %collective-permute-start.8 = (bf16[1,128,128]{2,1,0:T(8,128)(2,1)S(1)}, bf16[1,128,128]{2,1,0:T(8,128)(2,1)S(1)}, u32[]{:S(2)}, u32[]{:S(2)}) collective-permute-start(bf16[1,128,128]{2,1,0:T(8,128)(2,1)S(1)} %get-tuple-element.59), channel_id=1, source_target_pairs={{0,1},{1,2},{2,3},{3,4},{4,5},{5,6},{6,7},{7,8},{8,9},{9,10},{10,1... | collective-permute-start | bytes 98312 | tf_op jit(solution)/shard_map/ppermute | solution.py:11
  162.8 16.0 %collective-permute-start.9 = (bf16[1,128,128]{2,1,0:T(8,128)(2,1)S(1)}, bf16[1,128,128]{2,1,0:T(8,128)(2,1)S(1)}, u32[]{:S(2)}, u32[]{:S(2)}) collective-permute-start(bf16[1,128,128]{2,1,0:T(8,128)(2,1)S(1)} %get-tuple-element.59), channel_id=1, source_target_pairs={{1,0},{2,1},{3,2},{4,3},{5,4},{6,5},{7,6},{8,7},{9,8},{10,9},{11,1... | collective-permute-start | bytes 98312 | tf_op jit(solution)/shard_map/ppermute | solution.py:11
  164.7 22.8 %collective-permute-start.10 = (bf16[1,128,128]{2,1,0:T(8,128)(2,1)S(1)}, bf16[1,128,128]{2,1,0:T(8,128)(2,1)S(1)}, u32[]{:S(2)}, u32[]{:S(2)}) collective-permute-start(bf16[1,128,128]{2,1,0:T(8,128)(2,1)S(1)} %get-tuple-element.59), channel_id=1, source_target_pairs={{0,2},{1,3},{2,4},{3,5},{4,6},{5,7},{6,8},{7,9},{8,10},{9,11},{10,... | collective-permute-start | bytes 98312 | tf_op jit(solution)/shard_map/ppermute | solution.py:11
  170.1 18.8 %collective-permute-start.11 = (bf16[1,128,128]{2,1,0:T(8,128)(2,1)S(1)}, bf16[1,128,128]{2,1,0:T(8,128)(2,1)S(1)}, u32[]{:S(2)}, u32[]{:S(2)}) collective-permute-start(bf16[1,128,128]{2,1,0:T(8,128)(2,1)S(1)} %get-tuple-element.59), channel_id=1, source_target_pairs={{2,0},{3,1},{4,2},{5,3},{6,4},{7,5},{8,6},{9,7},{10,8},{11,9},{12,... | collective-permute-start | bytes 98312 | tf_op jit(solution)/shard_map/ppermute | solution.py:11
  171.4 17.5 %collective-permute-start.12 = (bf16[1,128,128]{2,1,0:T(8,128)(2,1)S(1)}, bf16[1,128,128]{2,1,0:T(8,128)(2,1)S(1)}, u32[]{:S(2)}, u32[]{:S(2)}) collective-permute-start(bf16[1,128,128]{2,1,0:T(8,128)(2,1)S(1)} %get-tuple-element.59), channel_id=1, source_target_pairs={{0,3},{1,4},{2,5},{3,6},{4,7},{5,8},{6,9},{7,10},{8,11},{9,12},{10... | collective-permute-start | bytes 98312 | tf_op jit(solution)/shard_map/ppermute | solution.py:11
  177.4 11.5 %collective-permute-start.13 = (bf16[1,128,128]{2,1,0:T(8,128)(2,1)S(1)}, bf16[1,128,128]{2,1,0:T(8,128)(2,1)S(1)}, u32[]{:S(2)}, u32[]{:S(2)}) collective-permute-start(bf16[1,128,128]{2,1,0:T(8,128)(2,1)S(1)} %get-tuple-element.59), channel_id=1, source_target_pairs={{3,0},{4,1},{5,2},{6,3},{7,4},{8,5},{9,6},{10,7},{11,8},{12,9},{13... | collective-permute-start | bytes 98312 | tf_op jit(solution)/shard_map/ppermute | solution.py:11
  178.7 10.2 %collective-permute-start.14 = (bf16[1,128,128]{2,1,0:T(8,128)(2,1)S(1)}, bf16[1,128,128]{2,1,0:T(8,128)(2,1)S(1)}, u32[]{:S(2)}, u32[]{:S(2)}) collective-permute-start(bf16[1,128,128]{2,1,0:T(8,128)(2,1)S(1)} %get-tuple-element.59), channel_id=1, source_target_pairs={{0,4},{1,5},{2,6},{3,7},{4,8},{5,9},{6,10},{7,11},{8,12},{9,13},{1... | collective-permute-start | bytes 98312 | tf_op jit(solution)/shard_map/ppermute | solution.py:11
  187.6 6.0 %collective-permute-start.15 = (bf16[1,128,128]{2,1,0:T(8,128)(2,1)S(1)}, bf16[1,128,128]{2,1,0:T(8,128)(2,1)S(1)}, u32[]{:S(2)}, u32[]{:S(2)}) collective-permute-start(bf16[1,128,128]{2,1,0:T(8,128)(2,1)S(1)} %get-tuple-element.59), channel_id=1, source_target_pairs={{4,0},{5,1},{6,2},{7,3},{8,4},{9,5},{10,6},{11,7},{12,8},{13,9},{1... | collective-permute-start | bytes 98312 | tf_op jit(solution)/shard_map/ppermute | solution.py:11
Sparse Core Ops, SparseCore 0:
  120.3 107.5 all-gather.1
